TPU v7x, 512 devices: a whole 4x4x16 slice. The times are simulated.
512 devices in a mesh: section: 2 (over x_hi), dp: 8 (over y, core), tensor: 32 (over x_lo, z).
Axes of the slice: x: 4 (x_hi: 2, x_lo: 2; x = x_hi * 2 + x_lo), y: 4, z: 16, core: 2. Of those that a mesh axis runs over, the one named last changes fastest.
Arguments:
- tokens_in: bfloat16 [2, 7168, 2048], P(None, 'tensor', 'dp'), may hold values from -47 to 47
- section_proj: bfloat16 [2, 7168, 7168], P('section', 'tensor'), may hold values from -0.0625 to 0.0625
- section_gain: bfloat16 [2, 7168], P('section', 'tensor'), may hold values from 0.099609375 to 1.8984375
- final_gain: bfloat16 [7168], P('tensor'), may hold values from 0.099609375 to 1.8984375
- score_weight: bfloat16 [7168], P('tensor'), may hold values from -0.0625 to 0.0625
- labels: int32 [2, 2048], P(None, 'dp'), may hold values from 0 to 2
- loss_mask: int32 [2, 2048], P(None, 'dp'), may hold values 0 or 1
- segment_ids: int32 [2, 2048], P(None, 'dp'), may hold values from 0 to 15, never falling along the last dimension, each value on 1 to 512 neighbouring positions
Outputs:
- section_out: bfloat16 [2, 2, 7168, 2048], P('section', None, 'tensor', 'dp')
- segment_loss: float32 [2, 16], replicated
Inputs may be any that keep to these rules, and one draw needn't show every extreme that they name: `segment_ids`: within a micro-batch segment numbers never fall along the tokens; each segment has 1 to 512 tokens.
All inputs are finite; a program needn't handle non-finite values. No bound on the sum of `loss_mask` on one device may be relied on, other than what follows from the above.
Results may differ from a plain program's by a relative error of at most 0.0045.
Values may be sent and summed in bfloat16 or wider, within the bound.
No kernel may reach another device: no remote copies, remote signals or barrier semaphores. Data moves between devices by JAX's collectives and lax.ppermute only.
A program may use at most 64 MiB of HBM per device.

v0:
```python
import jax
import jax.numpy as jnp
from jax import lax
from jax.sharding import PartitionSpec as P

D = 7168
SEGS = 16
epsilon = 1e-05


def passed_along(shard, axis, by):
    count = lax.axis_size(axis)
    pairs = [(i, i + by) for i in range(count) if 0 <= i + by < count]
    return lax.ppermute(shard, axis, pairs)


def body(
    tokens_in, section_proj, section_gain, final_gain, score_weight, labels, loss_mask, segment_ids
):
    section_index = lax.axis_index("section")
    weight_local = section_proj[0]
    gain_local = section_gain[0]
    head_vector = final_gain.astype(jnp.float32) * score_weight.astype(jnp.float32)
    micro_count = tokens_in.shape[0]
    received = jnp.zeros_like(tokens_in[0])
    produced = []
    score_list = []
    for moment in range(micro_count + 1):
        if moment < micro_count:
            fresh_rows = tokens_in[moment]
        else:
            fresh_rows = jnp.zeros_like(tokens_in[0])
        incoming = jnp.where(section_index == 0, fresh_rows, received)
        apply_as_float = incoming.astype(jnp.float32)
        apply_squares = lax.psum(jnp.sum(apply_as_float * apply_as_float, axis=0), "tensor")
        apply_inv_root = lax.rsqrt(apply_squares / D + epsilon)[None, :]
        normed = (apply_as_float * apply_inv_root * gain_local.astype(jnp.float32)[:, None]).astype(
            jnp.bfloat16
        )
        mixed = jnp.dot(
            weight_local,
            lax.all_gather(normed, "tensor", axis=0, tiled=True),
            preferred_element_type=jnp.float32,
        )
        result_rows = (apply_as_float + jax.nn.silu(mixed)).astype(jnp.bfloat16)
        produced.append(result_rows)
        if moment < micro_count:
            received = passed_along(result_rows, "section", 1)
        if moment >= 1:
            as_float = result_rows.astype(jnp.float32)
            squares_part = jnp.sum(as_float * as_float, axis=0)
            squares = lax.psum(squares_part, "tensor")
            inv_root = lax.rsqrt(squares / D + epsilon)
            partial_score = jnp.sum(as_float * inv_root[None, :] * head_vector[:, None], axis=0)
            score_list.append(lax.psum(partial_score, "tensor"))
    section_out = jnp.where(
        section_index == 0, jnp.stack(produced[:micro_count]), jnp.stack(produced[1:])
    )[None]
    segment_range = lax.broadcasted_iota(jnp.int32, (1, SEGS), 1)
    sum_rows = []
    count_rows = []
    for micro in range(micro_count):
        target = labels[micro].astype(jnp.float32) - 1.0
        weight_mask = loss_mask[micro].astype(jnp.float32)
        offset_err = score_list[micro] - target
        squared = weight_mask * offset_err * offset_err
        member = (segment_ids[micro][:, None] == segment_range).astype(jnp.float32)
        sum_rows.append(jnp.dot(squared, member, precision=lax.Precision.HIGHEST))
        count_rows.append(jnp.dot(weight_mask, member, precision=lax.Precision.HIGHEST))
    live_section = (section_index == 1).astype(jnp.float32)
    loss_sums, counted = lax.psum(
        (jnp.stack(sum_rows) * live_section, jnp.stack(count_rows) * live_section),
        ("section", "dp"),
    )
    segment_loss = loss_sums / jnp.maximum(counted, 1.0)
    return (section_out, segment_loss)


def solution(mesh):
    in_specs = (
        P(None, "tensor", "dp"),
        P("section", "tensor", None),
        P("section", "tensor"),
        P("tensor"),
        P("tensor"),
        P(None, "dp"),
        P(None, "dp"),
        P(None, "dp"),
    )
    out_specs = (P("section", None, "tensor", "dp"), P())
    return jax.shard_map(body, mesh=mesh, in_specs=in_specs, out_specs=out_specs, check_vma=False)
```

profile of v0, /device:TPU:1, one launch (start us, length us, event | category | flops | bytes accessed | tf_op | source)
XLA Modules:
  0.0 791.1 jit_solution(1438535462206001825)
XLA Ops:
  7.2 0.0 copy-start
  7.2 0.0 all-gather.4.cloned.1.call-start
  7.2 1.1 fusion.29
  8.3 57.2 %psum.63 = f32[256]{0:T(256)S(1)} all-reduce(f32[256]{0:T(256)S(1)} %fusion.29), channel_id=1, replica_groups=mesh['section'=2,'dp'=8,'tensor'=32] {'tensor'}, use_global_device_ids=true, to_apply=%region_1.2 | all-reduce | flops 256 | bytes 2048 | tf_op jit(solution)/shard_map/psum | solution.py:35
  65.5 0.7 convert_element_type.103
  66.2 0.0 copy-start.3
  66.2 0.5 copy-done.3
  66.8 1.6 fusion.31
  68.4 0.0 all-gather.4.cloned.1.call-update
  68.4 0.0 copy-start.1
  68.5 0.0 all-gather.6.cloned.1.call-start
  68.5 124.1 %all-gather.4.cloned.1.call-done = bf16[7168,256]{1,0:T(8,128)(2,1)} async-done(((bf16[224,256]{1,0:T(8,128)(2,1)}), bf16[7168,256]{1,0:T(8,128)(2,1)}) %all-gather.4.cloned.1.call-update) | async-done | bytes 3670032 | tf_op jit(solution)/shard_map/all_gather | solution.py:42
  192.6 0.0 copy-done
  192.6 3.1 fusion.32
  195.7 0.0 copy-start.2
  195.7 3.6 collective-permute-start
  199.3 2.0 collective-permute-done
  201.3 0.0 copy-done.1
  201.3 0.6 fusion.21
  201.9 0.0 copy-done.2
  201.9 49.3 %psum.64 = f32[256]{0:T(256)S(1)} all-reduce(f32[256]{0:T(256)} %get-tuple-element.10), channel_id=1, replica_groups=mesh['section'=2,'dp'=8,'tensor'=32] {'tensor'}, use_global_device_ids=true, to_apply=%region_3.4 | all-reduce | flops 256 | bytes 2048 | tf_op jit(solution)/shard_map/psum | solution.py:35
  251.2 1.4 fusion.23
  252.6 0.0 all-gather.6.cloned.1.call-update
  252.6 0.0 all-gather.8.cloned.1.call-start
  252.7 144.1 %all-gather.6.cloned.1.call-done = bf16[7168,256]{1,0:T(8,128)(2,1)} async-done(((bf16[224,256]{1,0:T(8,128)(2,1)}), bf16[7168,256]{1,0:T(8,128)(2,1)}) %all-gather.6.cloned.1.call-update) | async-done | bytes 3670032 | tf_op jit(solution)/shard_map/all_gather | solution.py:42
  396.8 3.6 fusion.15
  400.5 3.6 collective-permute-start.1
  404.1 2.0 collective-permute-done.1
  406.1 0.1 fusion.25
  406.1 49.3 %psum.65 = f32[256]{0:T(256)S(1)} all-reduce(f32[256]{0:T(256)S(1)} %fusion.25), channel_id=1, replica_groups=mesh['section'=2,'dp'=8,'tensor'=32] {'tensor'}, use_global_device_ids=true, to_apply=%region_5.6 | all-reduce | flops 256 | bytes 2048 | tf_op jit(solution)/shard_map/psum | solution.py:35
  455.4 1.4 fusion.27
  456.8 0.0 all-gather.8.cloned.1.call-update
  456.8 0.8 fusion.49
  457.6 0.0 copy-start.4
  457.6 0.0 copy-start.5
  457.6 0.5 copy-done.4
  458.1 0.9 fusion.39
  459.0 0.0 copy-done.5
  459.0 0.9 fusion.41
  460.0 0.6 maximum_multiply_fusion.1
  460.5 1.2 convert_multiply_fusion.10
  461.7 1.4 slice_convert_fusion.1
  463.1 1.4 convert_add_fusion.4
  464.5 136.4 %all-gather.8.cloned.1.call-done = bf16[7168,256]{1,0:T(8,128)(2,1)} async-done(((bf16[224,256]{1,0:T(8,128)(2,1)}), bf16[7168,256]{1,0:T(8,128)(2,1)}) %all-gather.8.cloned.1.call-update) | async-done | bytes 3670032 | tf_op jit(solution)/shard_map/all_gather | solution.py:42
  600.9 3.6 fusion.18
  604.5 48.4 %all-reduce.1 = (f32[256]{0:T(256)S(1)}, f32[256]{0:T(256)S(1)}) all-reduce(f32[256]{0:T(256)} %get-tuple-element.18, f32[256]{0:T(256)} %get-tuple-element.20), channel_id=1, replica_groups=mesh['section'=2,'dp'=8,'tensor'=32] {'tensor'}, use_global_device_ids=true, to_apply=%region_7.8 | all-reduce | flops 512 | bytes 4096 | tf_op jit(solution)/shard_map/psum | solution.py:52
  653.0 0.7 fusion.17
  653.7 46.4 %all-reduce = (f32[256]{0:T(256)S(1)}, f32[256]{0:T(256)S(1)}) all-reduce(f32[256]{0:T(256)S(1)} %get-tuple-element.3, f32[256]{0:T(256)S(1)} %get-tuple-element.2), channel_id=1, replica_groups=mesh['section'=2,'dp'=8,'tensor'=32] {'tensor'}, use_global_device_ids=true, to_apply=%region_13.14 | all-reduce | flops 512 | bytes 4096 | tf_op jit(solution)/shard_map/psum | solution.py:55
  700.1 0.7 multiply_multiply_fusion.1
  700.8 0.9 fusion.42
  701.6 0.7 multiply_multiply_fusion
  702.3 0.8 fusion.40
  703.2 79.2 %all-reduce.2 = (f32[2,16]{1,0:T(2,128)S(1)}, f32[2,16]{1,0:T(2,128)S(1)}) all-reduce(f32[2,16]{1,0:T(2,128)S(1)} %maximum_multiply_fusion, f32[2,16]{1,0:T(2,128)} %maximum_multiply_fusion.1), channel_id=1, replica_groups=mesh['section'=2,'dp'=8,'tensor'=32] {'section','dp'}, use_global_device_ids=true, to_apply=%region_14.15 | all-reduce | flops 64 | bytes 512 | tf_op jit(solution)/shard_map/psum | solution.py:71
  782.4 0.6 maximum_divide_fusion
  782.9 1.6 maximum_select_fusion
  (5 shorter events, 0.1 us)
Async XLA Ops:
  7.2 185.4 %copy-start = (bf16[1,224,7168]{2,1,0:T(8,128)(2,1)S(1)}, bf16[1,224,7168]{2,1,0:T(8,128)(2,1)}, u32[]{:S(2)}) copy-start(bf16[1,224,7168]{2,1,0:T(8,128)(2,1)} %param.9) | copy-start | bytes 9633796
  7.2 185.4 %all-gather.4.cloned.1.call-start = ((), (), s32[]{:S(2)}) async-start(), calls=%async_computation | async-start | bytes 3784704 | tf_op jit(solution)/shard_map/all_gather | solution.py:42
  66.2 0.5 copy-start.3
  68.4 132.9 %copy-start.1 = (bf16[2,224,256]{2,1,0:T(8,128)(2,1)S(1)}, bf16[2,224,256]{2,1,0:T(8,128)(2,1)}, u32[]{:S(2)}) copy-start(bf16[2,224,256]{2,1,0:T(8,128)(2,1)} %param.8) | copy-start | bytes 688132
  68.5 328.4 %all-gather.6.cloned.1.call-start = ((), (), s32[]{:S(2)}) async-start(), calls=%async_computation.1 | async-start | bytes 3784704 | tf_op jit(solution)/shard_map/all_gather | solution.py:42
  195.7 6.3 copy-start.2
  195.7 5.6 collective-permute-start
  252.6 348.3 %all-gather.8.cloned.1.call-start = ((), (), s32[]{:S(2)}) async-start(), calls=%async_computation.2 | async-start | bytes 3784704 | tf_op jit(solution)/shard_map/all_gather | solution.py:42
  400.5 5.6 collective-permute-start.1
  457.6 0.5 copy-start.4
  457.6 1.4 copy-start.5
Sparse Core Ops, SparseCore 0:
  68.6 123.9 all-gather.3
  252.7 144.0 all-gather.5
  456.9 143.8 all-gather.7
where the time goes:
time: 792 us; the launch traced here: 791 us
  waiting for transfers between devices  409 us (52%)
  blocking collectives  330 us (42%)
  other arithmetic  15.7 us (2%)
  matrix products  13.9 us (2%)
  between operations  13.8 us (2%)
    all_gather x3, waiting for transfers between devices, body(): lax.all_gather(normed, 'tensor', axis=0, tiled=True)  405 us
    psum x3, blocking collectives, body(): lax.psum(jnp.sum(apply_as_float * apply_as_float, axis=0), 'tensor')  156 us
    psum x1, blocking collectives, body(): lax.psum((jnp.stack(sum_rows) * live_section, jnp.stack(count_rows) * liv...  79.2 us
    psum x1, blocking collectives, body(): squares = lax.psum(squares_part, 'tensor')  48.4 us
    psum x1, blocking collectives, body(): score_list.append(lax.psum(partial_score, 'tensor'))  46.4 us
  transfers between devices with their start and end apart: 5, of which 5 were waited for; matrix products, arithmetic and copies ran while one was open for 1% of the time, Pallas kernels for 0%

commit v1 on v0

--- a/solution.py
+++ b/solution.py
@@ -1,3 +1,4 @@
+import functools
 import jax
 import jax.numpy as jnp
 from jax import lax
@@ -6,6 +7,22 @@
 D = 7168
 SEGS = 16
 epsilon = 1e-05
+
+
+def find_spots(local_values, mesh_ax):
+    later = jnp.concatenate(
+        jax.lax.all_to_all(
+            jnp.stack([local_values] * jax.lax.psum(1, axis_name=mesh_ax), axis=0),
+            axis_name=mesh_ax,
+            split_axis=0,
+            concat_axis=0,
+        ),
+        axis=0,
+    )
+    return later
+
+
+follow_meshes_here = functools.partial(find_spots, mesh_ax="tensor")
 
 
 def passed_along(shard, axis, by):
@@ -38,9 +55,7 @@
             jnp.bfloat16
         )
         mixed = jnp.dot(
-            weight_local,
-            lax.all_gather(normed, "tensor", axis=0, tiled=True),
-            preferred_element_type=jnp.float32,
+            weight_local, follow_meshes_here(normed), preferred_element_type=jnp.float32
         )
         result_rows = (apply_as_float + jax.nn.silu(mixed)).astype(jnp.bfloat16)
         produced.append(result_rows)

time: 792 us -> 808 us (1.020)
  blocking collectives: 330 us -> 683 us
  waiting for transfers between devices: 409 us -> 86.2 us
  between operations: 13.8 us -> 0.82 us
    all_gather x3 -> x0, waiting for transfers between devices: 405 us -> none  [body(): lax.all_gather(normed, 'tensor', axis=0, tiled=True)]
    all_to_all x0 -> x2, blocking collectives: none -> 280 us  [find_spots(): jax.lax.all_to_all(jnp.stack([local_values] * jax.lax.psum(1, axis_name=m...]
    all_to_all x0 -> x1, waiting for transfers between devices: none -> 81.8 us  [find_spots(): jax.lax.all_to_all(jnp.stack([local_values] * jax.lax.psum(1, axis_name=m...]
    psum x1, blocking collectives: 48.4 us -> 86.7 us  [body(): squares = lax.psum(squares_part, 'tensor')]
    psum x1, blocking collectives: 79.2 us -> 107 us  [body(): lax.psum((jnp.stack(sum_rows) * live_section, jnp.stack(count_rows) * liv...]
  transfers between devices with their start and end apart: 5 -> 3, of which waited for: 5 -> 3; matrix products, arithmetic and copies ran while one was open for 1% -> 0% of each run, Pallas kernels for 0% -> 0%
where the time goes in v1:
time: 808 us; the launch traced here: 807 us
  blocking collectives  683 us (85%)
  waiting for transfers between devices  86.2 us (11%)
  starting transfers between devices  14.7 us (2%)
  other arithmetic  10.6 us (1%)
  matrix products  8.57 us (1%)
    all_to_all x2, blocking collectives, find_spots(): jax.lax.all_to_all(jnp.stack([local_values] * jax.lax.psum(1, axis_name=m...  280 us
    psum x3, blocking collectives, body(): lax.psum(jnp.sum(apply_as_float * apply_as_float, axis=0), 'tensor')  163 us
    psum x1, blocking collectives, body(): lax.psum((jnp.stack(sum_rows) * live_section, jnp.stack(count_rows) * liv...  107 us
    psum x1, blocking collectives, body(): squares = lax.psum(squares_part, 'tensor')  86.7 us
    all_to_all x1, waiting for transfers between devices, find_spots(): jax.lax.all_to_all(jnp.stack([local_values] * jax.lax.psum(1, axis_name=m...  81.8 us
    psum x1, blocking collectives, body(): score_list.append(lax.psum(partial_score, 'tensor'))  46.3 us
  transfers between devices with their start and end apart: 3, of which 3 were waited for; matrix products, arithmetic and copies ran while one was open for 0% of the time, Pallas kernels for 0%

profile of v1, /device:TPU:1, one launch (start us, length us, event | category | flops | bytes accessed | tf_op | source)
XLA Modules:
  0.0 807.1 jit_solution(9101060022060152495)
XLA Ops:
  0.6 0.0 copy-start
  0.7 1.1 fusion.23
  1.8 57.2 %psum.63 = f32[256]{0:T(256)S(1)} all-reduce(f32[256]{0:T(256)S(1)} %fusion.23), channel_id=1, replica_groups=mesh['section'=2,'dp'=8,'tensor'=32] {'tensor'}, use_global_device_ids=true, to_apply=%region_1.2 | all-reduce | flops 256 | bytes 2048 | tf_op jit(solution)/shard_map/psum | solution.py:52
  59.0 0.7 convert_element_type.108
  59.7 0.0 copy-start.3
  59.7 1.0 fusion.45
  60.7 0.4 stack.31
  61.1 0.0 copy-start.1
  61.1 151.5 %all_to_all.15 = bf16[32,224,256]{2,1,0:T(8,128)(2,1)S(1)} all-to-all(bf16[32,224,256]{2,1,0:T(8,128)(2,1)S(1)} %stack.31), channel_id=1, replica_groups=mesh['section'=2,'dp'=8,'tensor'=32] {'tensor'}, dimensions={0} | all-to-all | bytes 7340032 | tf_op jit(solution)/shard_map/all_to_all | solution.py:14
  212.5 0.0 copy-done
  212.5 0.0 copy-done.1
  212.6 1.1 fusion.24
  213.6 0.0 copy-start.2
  213.6 4.4 collective-permute-start
  218.0 2.4 collective-permute-done
  220.4 0.1 fusion.27
  220.5 50.6 %psum.64 = f32[256]{0:T(256)S(1)} all-reduce(f32[256]{0:T(256)S(1)} %get-tuple-element.10), channel_id=1, replica_groups=mesh['section'=2,'dp'=8,'tensor'=32] {'tensor'}, use_global_device_ids=true, to_apply=%region_3.4 | all-reduce | flops 256 | bytes 2048 | tf_op jit(solution)/shard_map/psum | solution.py:52
  271.0 0.0 copy-done.2
  271.0 0.0 copy-done.3
  271.0 0.1 fusion.29
  271.1 0.4 stack.33
  271.6 128.8 %all_to_all.16 = bf16[32,224,256]{2,1,0:T(8,128)(2,1)S(1)} all-to-all(bf16[32,224,256]{2,1,0:T(8,128)(2,1)S(1)} %stack.33), channel_id=1, replica_groups=mesh['section'=2,'dp'=8,'tensor'=32] {'tensor'}, dimensions={0} | all-to-all | bytes 7340032 | tf_op jit(solution)/shard_map/all_to_all | solution.py:14
  400.4 1.7 fusion.17
  402.0 5.4 collective-permute-start.1
  407.4 2.1 collective-permute-done.1
  409.4 0.1 fusion.31
  409.5 55.4 %psum.65 = f32[256]{0:T(256)S(1)} all-reduce(f32[256]{0:T(256)S(1)} %fusion.31), channel_id=1, replica_groups=mesh['section'=2,'dp'=8,'tensor'=32] {'tensor'}, use_global_device_ids=true, to_apply=%region_5.6 | all-reduce | flops 256 | bytes 2048 | tf_op jit(solution)/shard_map/psum | solution.py:52
  464.9 0.8 fusion.33
  465.7 2.2 stack.36
  468.0 0.0 copy-start.4
  468.0 0.0 copy-start.5
  468.0 0.0 copy-start.9
  468.0 0.0 copy-start.10
  468.0 0.0 copy-start.6
  468.0 5.0 all-to-all-start.2
  473.0 0.0 copy-done.4
  473.0 0.0 copy-start.7
  473.0 0.0 copy-start.8
  473.0 0.0 copy-done.5
  473.0 0.2 fusion.41
  473.2 0.2 fusion.43
  473.5 0.6 maximum_multiply_fusion.1
  474.1 0.0 copy-done.9
  474.1 0.0 copy-done.10
  474.1 0.6 convert_multiply_fusion.9
  474.7 0.6 slice_convert_fusion.1
  475.3 0.0 copy-done.6
  475.3 0.6 convert_add_fusion.3
  475.9 81.8 %all-to-all-done.2 = bf16[32,224,256]{2,1,0:T(8,128)(2,1)} async-done(((bf16[32,224,256]{2,1,0:T(8,128)(2,1)}), bf16[32,224,256]{2,1,0:T(8,128)(2,1)}, u32[]{:S(2)}, u32[]{:S(2)}) %all-to-all-start.2) | async-done | bytes 3670048 | tf_op jit(solution)/shard_map/all_to_all | solution.py:14
  557.6 0.0 copy-done.7
  557.6 0.0 copy-done.8
  557.6 3.6 fusion.20
  561.3 86.7 %all-reduce.1 = (f32[256]{0:T(256)S(1)}, f32[256]{0:T(256)S(1)}) all-reduce(f32[256]{0:T(256)} %get-tuple-element.18, f32[256]{0:T(256)} %get-tuple-element.20), channel_id=1, replica_groups=mesh['section'=2,'dp'=8,'tensor'=32] {'tensor'}, use_global_device_ids=true, to_apply=%region_7.8 | all-reduce | flops 512 | bytes 4096 | tf_op jit(solution)/shard_map/psum | solution.py:67
  648.0 0.8 fusion.19
  648.8 46.3 %all-reduce = (f32[256]{0:T(256)S(1)}, f32[256]{0:T(256)S(1)}) all-reduce(f32[256]{0:T(256)S(1)} %get-tuple-element.3, f32[256]{0:T(256)S(1)} %get-tuple-element.2), channel_id=1, replica_groups=mesh['section'=2,'dp'=8,'tensor'=32] {'tensor'}, use_global_device_ids=true, to_apply=%region_13.14 | all-reduce | flops 512 | bytes 4096 | tf_op jit(solution)/shard_map/psum | solution.py:70
  695.1 0.7 multiply_multiply_fusion.1
  695.8 0.9 fusion.44
  696.7 0.7 multiply_multiply_fusion
  697.4 0.9 fusion.42
  698.3 106.7 %all-reduce.2 = (f32[2,16]{1,0:T(2,128)S(1)}, f32[2,16]{1,0:T(2,128)S(1)}) all-reduce(f32[2,16]{1,0:T(2,128)S(1)} %maximum_multiply_fusion, f32[2,16]{1,0:T(2,128)} %maximum_multiply_fusion.1), channel_id=1, replica_groups=mesh['section'=2,'dp'=8,'tensor'=32] {'section','dp'}, use_global_device_ids=true, to_apply=%region_14.15 | all-reduce | flops 64 | bytes 512 | tf_op jit(solution)/shard_map/psum | solution.py:86
  804.9 0.6 maximum_divide_fusion
  805.5 1.6 maximum_select_fusion
  (6 shorter events, 0.1 us)
Async XLA Ops:
  0.6 211.9 %copy-start = (bf16[1,224,7168]{2,1,0:T(8,128)(2,1)S(1)}, bf16[1,224,7168]{2,1,0:T(8,128)(2,1)}, u32[]{:S(2)}) copy-start(bf16[1,224,7168]{2,1,0:T(8,128)(2,1)} %param.9) | copy-start | bytes 9633796
  59.7 211.4 %copy-start.3 = (f32[1,224]{1,0:T(1,128)}, f32[1,224]{1,0:T(1,128)S(1)}, u32[]{:S(2)}) copy-start(f32[1,224]{1,0:T(1,128)S(1)} %convert_element_type.108) | copy-start | bytes 2692
  61.1 151.5 %copy-start.1 = (bf16[2,224,256]{2,1,0:T(8,128)(2,1)S(1)}, bf16[2,224,256]{2,1,0:T(8,128)(2,1)}, u32[]{:S(2)}) copy-start(bf16[2,224,256]{2,1,0:T(8,128)(2,1)} %param.8) | copy-start | bytes 688132
  213.6 57.4 %copy-start.2 = (bf16[224,256]{1,0:T(8,128)(2,1)}, bf16[224,256]{1,0:T(8,128)(2,1)S(1)}, u32[]{:S(2)}) copy-start(bf16[224,256]{1,0:T(8,128)(2,1)S(1)} %fusion.24) | copy-start | bytes 344068
  213.6 6.8 collective-permute-start
  402.0 7.4 collective-permute-start.1
  468.0 5.0 copy-start.4
  468.0 5.0 copy-start.5
  468.0 6.1 copy-start.9
  468.0 6.1 copy-start.10
  468.0 7.3 copy-start.6
  468.0 89.6 %all-to-all-start.2 = ((bf16[32,224,256]{2,1,0:T(8,128)(2,1)}), bf16[32,224,256]{2,1,0:T(8,128)(2,1)}, u32[]{:S(2)}, u32[]{:S(2)}) async-start(bf16[32,224,256]{2,1,0:T(8,128)(2,1)} %stack.36), calls=%async_computation.2 | async-start | bytes 7340032 | tf_op jit(solution)/shard_map/all_to_all | solution.py:14
  473.0 84.6 %copy-start.7 = (s32[1,256]{1,0:T(1,128)}, s32[1,256]{1,0:T(1,128)S(1)}, u32[]{:S(2)}) copy-start(s32[1,256]{1,0:T(1,128)S(1)} %get-tuple-element.13) | copy-start | bytes 3076
  473.0 84.6 %copy-start.8 = (s32[1,256]{1,0:T(1,128)}, s32[1,256]{1,0:T(1,128)S(1)}, u32[]{:S(2)}) copy-start(s32[1,256]{1,0:T(1,128)S(1)} %get-tuple-element.12) | copy-start | bytes 3076
